TPU v7x, 128 devices: a whole 4x4x4 slice. The times are simulated.
128 devices in a mesh: expert: 16 (over y, x_lo, core), tensor: 8 (over x_hi, z).
Axes of the slice: x: 4 (x_hi: 2, x_lo: 2; x = x_hi * 2 + x_lo), y: 4, z: 4, core: 2. Of those that a mesh axis runs over, the one named last changes fastest.
Arguments:
- tokens: bfloat16 [4096, 7168], P(('expert', 'tensor')), may hold values from -6 to 6
- expert_ids: int32 [4096, 2], P('expert'), may hold values from 0 to 2, all different within a row
- gate_scores: int32 [4096, 2], P('expert'), may hold values from 1 to 64
- gate_weight: bfloat16 [3, 7168, 2048], P(None, ('expert', 'tensor')), may hold values from -0.0625 to 0.0625
- up_weight: bfloat16 [3, 7168, 2048], P(None, ('expert', 'tensor')), may hold values from -0.0625 to 0.0625
- down_weight: bfloat16 [3, 7168, 2048], P(None, ('expert', 'tensor')), may hold values from -0.1875 to 0.1875
Outputs:
- mixed: bfloat16 [4096, 7168], P(('expert', 'tensor'))
Inputs may be any that keep to these rules, and one draw needn't show every extreme that they name: `expert_ids`: each row names 2 different experts.
All inputs are finite; a program needn't handle non-finite values.
Results may differ from a plain program's by a relative error of at most 0.015.
Values may be sent and summed in bfloat16 or wider, within the bound.
A program may use at most 128 MiB of HBM per device.

v0:
```python
import jax
import jax.numpy as jnp
from jax import lax
from jax.sharding import PartitionSpec as P


def activate(gate_sum, up_sum, weight_col):
    return (jax.nn.silu(gate_sum) * up_sum * weight_col).astype(jnp.bfloat16)


def local(tokens, expert_ids, gate_scores, gate_weight, up_weight, down_weight):
    gathered = lax.all_gather(tokens, "tensor", axis=0, tiled=True)
    experts = gate_weight.shape[0]
    scores = gate_scores.astype(jnp.float32)
    score_sum = jnp.sum(scores, axis=1, keepdims=True)
    labels = jnp.arange(experts, dtype=jnp.int32)
    picked = (expert_ids[:, :, None] == labels[None, None, :]).astype(jnp.float32)
    combine = jnp.sum(scores[:, :, None] * picked, axis=1) / score_sum
    served_gate, served_up, served_down = (
        lax.all_to_all(gate_weight, "tensor", split_axis=2, concat_axis=1, tiled=True),
        lax.all_to_all(up_weight, "tensor", split_axis=2, concat_axis=1, tiled=True),
        lax.all_to_all(down_weight, "tensor", split_axis=2, concat_axis=1, tiled=True),
    )
    hiddens = []
    full_gate, full_up = (
        lax.all_gather(served_gate, "expert", axis=1, tiled=True),
        lax.all_gather(served_up, "expert", axis=1, tiled=True),
    )
    for which in range(experts):
        gate_sum = jnp.dot(gathered, full_gate[which], preferred_element_type=jnp.float32)
        up_sum = jnp.dot(gathered, full_up[which], preferred_element_type=jnp.float32)
        hiddens.append(activate(gate_sum, up_sum, combine[:, which : which + 1]))
    stacked = jnp.stack(hiddens)
    partial_sum = jnp.einsum(
        "etf,edf->td",
        stacked,
        lax.all_gather(served_down, "expert", axis=1, tiled=True),
        preferred_element_type=jnp.float32,
    )
    output_rows = lax.psum_scatter(
        partial_sum.astype(jnp.bfloat16), "tensor", scatter_dimension=0, tiled=True
    )
    return output_rows


def solution(mesh):
    return jax.shard_map(
        local,
        mesh=mesh,
        in_specs=(
            P(("expert", "tensor"), None),
            P("expert", None),
            P("expert", None),
            P(None, ("expert", "tensor"), None),
            P(None, ("expert", "tensor"), None),
            P(None, ("expert", "tensor"), None),
        ),
        out_specs=P(("expert", "tensor"), None),
        check_vma=False,
    )
```

profile of v0, /device:TPU:1, one launch (start us, length us, event | category | flops | bytes accessed | tf_op | source)
XLA Modules:
  0.0 392.6 jit_solution(62899333029683740)
XLA Ops:
  6.5 0.7 all-gather.5.cloned.1.call-update
  7.3 0.0 all-gather.7.cloned.1.call-start
  7.3 2.8 copy.28
  10.1 2.7 reshape.8
  12.8 23.3 %all_to_all.54 = bf16[8,2,21504]{2,1,0:T(2,128)(2,1)S(1)} all-to-all(bf16[8,2,21504]{2,1,0:T(2,128)(2,1)S(1)} %reshape.8), channel_id=1, replica_groups=mesh['expert'=16,'tensor'=8] {'tensor'}, dimensions={0} | all-to-all | bytes 1376256 | tf_op jit(solution)/shard_map/all_to_all | solution.py:20
  36.2 3.0 reshape.9
  39.2 2.1 copy.37
  41.4 0.0 all-gather.9.cloned.1.call-start
  41.4 1.4 copy.31
  42.8 2.7 reshape.6
  45.5 14.1 %all_to_all.55 = bf16[8,2,21504]{2,1,0:T(2,128)(2,1)S(1)} all-to-all(bf16[8,2,21504]{2,1,0:T(2,128)(2,1)S(1)} %reshape.6), channel_id=1, replica_groups=mesh['expert'=16,'tensor'=8] {'tensor'}, dimensions={0} | all-to-all | bytes 1376256 | tf_op jit(solution)/shard_map/all_to_all | solution.py:21
  59.6 3.0 reshape.7
  62.6 2.2 copy.39
  64.8 0.0 all-gather.11.cloned.1.call-start
  64.8 1.4 copy.34
  66.2 2.7 reshape.4
  68.9 16.3 %all_to_all.56 = bf16[8,2,21504]{2,1,0:T(2,128)(2,1)S(1)} all-to-all(bf16[8,2,21504]{2,1,0:T(2,128)(2,1)S(1)} %reshape.4), channel_id=1, replica_groups=mesh['expert'=16,'tensor'=8] {'tensor'}, dimensions={0} | all-to-all | bytes 1376256 | tf_op jit(solution)/shard_map/all_to_all | solution.py:22
  85.2 3.0 reshape.5
  88.2 2.2 copy.35
  90.4 0.2 reduce-scatter.2.cloned.1.call-start
  90.7 3.6 all-gather.5.cloned.1.call-done
  94.4 63.5 %all-gather.7.cloned.1.call-done = bf16[3,7168,256]{2,1,0:T(8,128)(2,1)} async-done(((bf16[3,448,256]{2,1,0:T(8,128)(2,1)}), bf16[3,7168,256]{2,1,0:T(8,128)(2,1)}) %all-gather.7.cloned.1.call-update) | async-done | bytes 11010064 | tf_op jit(solution)/shard_map/all_gather | solution.py:26
  157.9 4.4 %fusion.2 = f32[256,256]{1,0:T(8,128)S(1)} fusion(bf16[256,7168]{1,0:T(8,128)(2,1)} %all-gather.5.cloned.1.call-done, bf16[3,7168,256]{2,1,0:T(8,128)(2,1)} %all-gather.7.cloned.1.call-done), kind=kOutput, calls=%fused_computation.5 | convolution fusion | flops 939524096 | bytes 7602176 | tf_op jit(solution)/shard_map/dot_general | solution.py:30
  162.3 3.2 fusion.4
  165.5 3.2 fusion.6
  168.7 56.2 %all-gather.9.cloned.1.call-done = bf16[3,7168,256]{2,1,0:T(8,128)(2,1)} async-done(((bf16[3,448,256]{2,1,0:T(8,128)(2,1)}), bf16[3,7168,256]{2,1,0:T(8,128)(2,1)}) %all-gather.9.cloned.1.call-update) | async-done | bytes 11010064 | tf_op jit(solution)/shard_map/all_gather | solution.py:27
  225.0 4.4 %fusion.18 = bf16[1,256,256]{2,1,0:T(8,128)(2,1)S(1)} fusion(bf16[256,7168]{1,0:T(8,128)(2,1)} %all-gather.5.cloned.1.call-done, bf16[3,7168,256]{2,1,0:T(8,128)(2,1)} %all-gather.9.cloned.1.call-done, f32[256,256]{1,0:T(8,128)S(1)} %fusion.2, f32[256]{0:T(256)S(1)} %bitcast.93), kind=kOutput, calls=%fused_computation.25 | convolution fusion | flops 939982848 | bytes 7734272 | tf_op jit(solution)/shard_map/dot_general | solution.py:31
  229.4 3.2 fusion.17
  232.6 3.2 fusion.16
  235.8 56.2 %all-gather.11.cloned.1.call-done = bf16[3,7168,256]{2,1,0:T(8,128)(2,1)} async-done(((bf16[3,448,256]{2,1,0:T(8,128)(2,1)}), bf16[3,7168,256]{2,1,0:T(8,128)(2,1)}) %all-gather.11.cloned.1.call-update) | async-done | bytes 11010064 | tf_op jit(solution)/shard_map/all_gather | solution.py:37
  291.9 12.5 %fusion = bf16[256,7168]{1,0:T(8,128)(2,1)} fusion(bf16[3,7168,256]{2,1,0:T(8,128)(2,1)} %all-gather.11.cloned.1.call-done, bf16[1,256,256]{2,1,0:T(8,128)(2,1)S(1)} %fusion.18, bf16[1,256,256]{2,1,0:T(8,128)(2,1)S(1)} %fusion.17, bf16[1,256,256]{2,1,0:T(8,128)(2,1)S(1)} %fusion.16), kind=kOutput, calls=%fused_computation.1 | convolution fusion | flops 2820800512 | bytes 15073280 | tf_op jit(solution)/shard_map/etf,edf->td/dot_general | solution.py:34
  304.5 81.6 %reduce-scatter.2.cloned.1.call-done = bf16[32,7168]{1,0:T(8,128)(2,1)} async-done(((bf16[256,7168]{1,0:T(8,128)(2,1)}), bf16[32,7168]{1,0:T(8,128)(2,1)}) %reduce-scatter.2.cloned.1.call-update) | async-done | bytes 458768 | tf_op jit(solution)/shard_map/reduce_scatter | solution.py:40
  (22 shorter events, 0.2 us)
Async XLA Ops:
  6.5 87.8 %all-gather.5.cloned.1.call-start = ((), (), s32[]{:S(2)}) async-start(), calls=%async_computation.4 | async-start | bytes 4128768 | tf_op jit(solution)/shard_map/all_gather | solution.py:12
  7.3 150.6 %all-gather.7.cloned.1.call-start = ((), (), s32[]{:S(2)}) async-start(), calls=%async_computation.5 | async-start | bytes 11698176 | tf_op jit(solution)/shard_map/all_gather | solution.py:26
  36.2 5.2 %copy-start = (bf16[3,56,2048]{2,1,0:T(8,128)(2,1)S(1)}, bf16[3,56,2048]{2,1,0:T(8,128)(2,1)}, u32[]{:S(2)}) copy-start(bf16[3,56,2048]{2,1,0:T(8,128)(2,1)} %param.10) | copy-start | bytes 2064388
  41.4 183.6 %all-gather.9.cloned.1.call-start = ((), (), s32[]{:S(2)}) async-start(), calls=%async_computation.6 | async-start | bytes 11698176 | tf_op jit(solution)/shard_map/all_gather | solution.py:27
  59.6 5.3 %copy-start.1 = (bf16[3,56,2048]{2,1,0:T(8,128)(2,1)S(1)}, bf16[3,56,2048]{2,1,0:T(8,128)(2,1)}, u32[]{:S(2)}) copy-start(bf16[3,56,2048]{2,1,0:T(8,128)(2,1)} %param.11) | copy-start | bytes 2064388
  64.8 227.1 %all-gather.11.cloned.1.call-start = ((), (), s32[]{:S(2)}) async-start(), calls=%async_computation.7 | async-start | bytes 11698176 | tf_op jit(solution)/shard_map/all_gather | solution.py:37
  68.9 21.7 %copy-start.2 = (s32[256,2]{0,1:T(2,128)S(1)}, s32[256,2]{0,1:T(2,128)}, u32[]{:S(2)}) copy-start(s32[256,2]{0,1:T(2,128)} %param.8) | copy-start | bytes 6148
  68.9 21.8 %copy-start.3 = (s32[256,2]{0,1:T(2,128)S(1)}, s32[256,2]{0,1:T(2,128)}, u32[]{:S(2)}) copy-start(s32[256,2]{0,1:T(2,128)} %param.7) | copy-start | bytes 6148
  90.4 295.6 %reduce-scatter.2.cloned.1.call-start = ((), (), s32[]{:S(2)}) async-start(), calls=%async_computation.8 | async-start | bytes 4128768 | tf_op jit(solution)/shard_map/reduce_scatter | solution.py:40
  157.9 4.4 %copy-start.4 = (bf16[256,7168]{1,0:T(8,128)(2,1)S(1)}, bf16[256,7168]{1,0:T(8,128)(2,1)}, u32[]{:S(2)}) copy-start(bf16[256,7168]{1,0:T(8,128)(2,1)} %all-gather.5.cloned.1.call-done) | copy-start | bytes 11010052
  225.0 4.4 %copy-start.5 = (bf16[256,7168]{1,0:T(8,128)(2,1)S(1)}, bf16[256,7168]{1,0:T(8,128)(2,1)}, u32[]{:S(2)}) copy-start(bf16[256,7168]{1,0:T(8,128)(2,1)} %all-gather.5.cloned.1.call-done) | copy-start | bytes 11010052
Sparse Core Ops, SparseCore 0:
  9.7 84.6 all-gather.4
  96.0 61.7 all-gather.6
  159.5 65.3 all-gather.8
  226.5 65.3 all-gather.10
  304.6 81.4 reduce-scatter.1
where the time goes:
time: 394 us; the launch traced here: 393 us
  waiting for transfers between devices  262 us (66%)
  blocking collectives  53.7 us (14%)
  matrix products  34.1 us (9%)
  local copies, waits for them, and re-layouts  29.2 us (7%)
  between operations  13.3 us (3%)
    reduce_scatter x1, waiting for transfers between devices, local(): lax.psum_scatter(partial_sum.astype(jnp.bfloat16), 'tensor', scatter_dime...  81.6 us
    all_gather x1, waiting for transfers between devices, local(): lax.all_gather(served_gate, 'expert', axis=1, tiled=True)  63.5 us
    all_gather x1, waiting for transfers between devices, local(): lax.all_gather(served_up, 'expert', axis=1, tiled=True)  56.2 us
    all_gather x1, waiting for transfers between devices, local(): lax.all_gather(served_down, 'expert', axis=1, tiled=True)  56.2 us
    all_to_all x1, blocking collectives, local(): lax.all_to_all(gate_weight, 'tensor', split_axis=2, concat_axis=1, tiled=...  23.3 us
    unnamed x21, local copies, waits for them, and re-layouts  22.7 us
    all_to_all x1, blocking collectives, local(): lax.all_to_all(down_weight, 'tensor', split_axis=2, concat_axis=1, tiled=...  16.3 us
    all_to_all x1, blocking collectives, local(): lax.all_to_all(up_weight, 'tensor', split_axis=2, concat_axis=1, tiled=True)  14.1 us
  transfers between devices with their start and end apart: 5, of which 5 were waited for; matrix products, arithmetic and copies ran while one was open for 13% of the time, Pallas kernels for 0%

commit v1 on v0

v1 whole, which is shorter than its diff:
```python
import jax
import jax.numpy as jnp
from jax import lax
from jax.experimental import pallas as pl
from jax.experimental.pallas import tpu as pltpu
from jax.sharding import PartitionSpec as P

MESH = pl.DeviceIdType.MESH
F32 = jnp.float32
BF16 = jnp.bfloat16

N = 4
EXPERTS = 3
D = 7168
ROWS = 32
DEPTH = 56
CHUNK = 448
QUARTER = 1792
UNITS = 128
HALF = D // 2
PIECES = 8
WIDE = D // PIECES

PLANE = (
    (1, 0), (3, 0), (0, 1), (0, 3), (2, 0), (0, 2), (1, 1), (3, 3),
    (2, 1), (1, 3), (3, 1), (2, 3), (1, 2), (3, 2), (2, 2),
)


def place():
    e = lax.axis_index("expert")
    t = lax.axis_index("tensor")
    y, xl, c = lax.div(e, 4), lax.rem(lax.div(e, 2), 2), lax.rem(e, 2)
    xh, z = lax.div(t, 4), lax.rem(t, 4)
    return e, t, y, xh * 2 + xl, z, c, xl, xh


def device(y, x, z, c):
    return {
        "expert": y * 4 + lax.rem(x, 2) * 2 + c,
        "tensor": lax.div(x, 2) * 4 + z,
    }


def ring(v, d):
    return lax.rem(v + d, N)


def kernel(
    tok, ids, scores, gate, up, down, out,
    xs, ws, acc, hid, part, r1, s1, r2, comb,
    ssem, asend, arecv, wrecv, trecv, crecv, rrecv1, rrecv2, lsem,
):
    e, t, y, x, z, c, xl, xh = place()
    mine = e * 8 + t
    sends = []

    def send(src, dst, recv, to):
        cp = pltpu.make_async_remote_copy(
            src_ref=src,
            dst_ref=dst,
            send_sem=ssem.at[len(sends)],
            recv_sem=recv,
            device_id=to,
            device_id_type=MESH,
        )
        cp.start()
        sends.append(cp)

    def arrived(ref, sem):
        pltpu.make_async_copy(ref, ref, sem).wait()

    which = lax.broadcasted_iota(jnp.int32, (8, 256), 0)
    marks = scores[...].astype(F32)
    first, second = marks[0:1, :], marks[1:2, :]
    picked = jnp.where(ids[0:1, :] == which, first, 0.0) + jnp.where(
        ids[1:2, :] == which, second, 0.0
    )
    comb[xl] = picked / (first + second)

    barrier = pltpu.get_barrier_semaphore()
    peers = [device(y, ring(x, dx), ring(z, dz), c) for dx, dz in PLANE]
    north, south = device(ring(y, 1), x, z, c), device(ring(y, 3), x, z, c)
    partner = device(y, x, z, 1 - c)
    for to in [*peers, north, south, partner]:
        pl.semaphore_signal(barrier, inc=1, device_id=to, device_id_type=MESH)
    pl.semaphore_wait(barrier, len(peers) + 3)

    own_rows = pl.ds(pl.multiple_of(mine * DEPTH, 8), DEPTH)

    def columns(px, pz):
        return pl.ds(pl.multiple_of((px * N + pz) * UNITS, UNITS), UNITS)

    def spread(ref, lo, kind):
        for (dx, dz), to in zip(PLANE, peers):
            cols = columns(ring(x, dx), ring(z, dz))
            pltpu.make_async_remote_copy(
                src_ref=ref.at[:, :, cols],
                dst_ref=ws.at[lo : lo + EXPERTS, own_rows, :],
                send_sem=asend.at[kind],
                recv_sem=arecv.at[kind, xl],
                device_id=to,
                device_id_type=MESH,
            ).start()

    def keep(ref, lo, kind):
        pltpu.make_async_copy(
            ref.at[:, :, columns(x, z)],
            ws.at[lo : lo + EXPERTS, own_rows, :],
            arecv.at[kind, xl],
        ).start()

    h0, h1 = pl.ds(0, HALF), pl.ds(HALF, HALF)
    own_tok = pltpu.make_async_copy(tok, xs.at[x, z], lsem)
    own_tok.start()
    keep(gate, 0, 0)
    keep(up, 3, 0)
    keep(down, 6, 1)
    spread(gate, 0, 0)
    spread(up, 3, 0)
    other = device(y, xh * 2 + 1 - xl, z, c)
    send(comb.at[xl], comb.at[xl], crecv, other)

    def along(axis, d):
        if axis == 0:
            return device(y, ring(x, d), z, c)
        return device(y, x, ring(z, d), c)

    def send_tokens(src, bx, bz, half, axis):
        cols = (h0, h1)[half]
        for d in (1, 3, 2):
            send(src, xs.at[bx, bz, :, cols], trecv.at[half, bx, bz], along(axis, d))

    send_tokens(tok.at[:, h0], x, z, 0, 0)
    send_tokens(tok.at[:, h1], x, z, 1, 1)
    send_tokens(tok.at[:, h0], x, z, 0, 1)
    send_tokens(tok.at[:, h1], x, z, 1, 0)
    spread(down, 6, 1)

    bounds = ((0, 6), (6, 9))

    def chunk(kind, cy, cx, cc):
        lo, hi = bounds[kind]
        k = cy * 4 + cx * 2 + cc
        rows = pl.ds(pl.multiple_of(k * CHUNK, CHUNK), CHUNK)
        return ws.at[lo:hi, rows, :], wrecv.at[kind, k]

    def pass_on(kind, cy, cx, to):
        ref, sem = chunk(kind, cy, cx, c)
        send(ref, ref, sem, to)

    def wait_chunk(kind, cy, cx, cc):
        ref, sem = chunk(kind, cy, cx, cc)
        arrived(ref, sem)

    def own_chunks(kind):
        arrived(chunk(kind, y, 0, c)[0], arecv.at[kind, 0])
        pass_on(kind, y, 0, north)
        pass_on(kind, y, 0, partner)
        arrived(chunk(kind, y, 1, c)[0], arecv.at[kind, 1])
        pass_on(kind, y, 1, south)
        pass_on(kind, y, 1, north)
        pass_on(kind, y, 0, south)
        pass_on(kind, y, 1, partner)

    before, after, across = ring(y, 3), ring(y, 1), ring(y, 2)

    def relay(kind):
        wait_chunk(kind, before, 0, c)
        pass_on(kind, before, 0, north)
        pass_on(kind, before, 0, partner)
        wait_chunk(kind, after, 1, c)
        pass_on(kind, after, 1, south)
        pass_on(kind, after, 1, partner)

    def hand_over(kind):
        wait_chunk(kind, before, 1, c)
        pass_on(kind, before, 1, partner)
        wait_chunk(kind, after, 0, c)
        pass_on(kind, after, 0, partner)

    def hand_over_far(kind):
        for cx in range(2):
            wait_chunk(kind, across, cx, c)
            pass_on(kind, across, cx, partner)

    def from_partner(kind, cy):
        for cx in range(2):
            wait_chunk(kind, cy, cx, 1 - c)

    def wait_tokens(bx, bz, half):
        arrived(xs.at[bx, bz, :, (h0, h1)[half]], trecv.at[half, bx, bz])

    own_chunks(0)
    for d in (3, 1, 2):
        bx = ring(x, d)
        wait_tokens(bx, z, 0)
        send_tokens(xs.at[bx, z, :, h0], bx, z, 0, 1)
        bz = ring(z, d)
        wait_tokens(x, bz, 1)
        send_tokens(xs.at[x, bz, :, h1], x, bz, 1, 0)
    relay(0)
    own_chunks(1)
    hand_over(0)
    own_tok.wait()
    for bd in range(1, N):
        for ad in range(N):
            wait_tokens(ring(x, ad), ring(z, bd), 0)
            wait_tokens(ring(x, bd), ring(z, ad), 1)

    def products(cy, start):
        span = pl.ds(pl.multiple_of(cy * QUARTER, 256), QUARTER)

        def one(w, carry):
            left = xs[:, :, :, span].reshape(N * N * ROWS, QUARTER)
            right = jnp.concatenate([ws[w, span, :], ws[EXPERTS + w, span, :]], axis=1)
            total = jnp.dot(left, right, preferred_element_type=F32)
            acc[w] = total if start else acc[w] + total
            return carry

        lax.fori_loop(0, EXPERTS, one, 0)

    from_partner(0, y)
    products(y, True)
    from_partner(0, before)
    products(before, False)
    from_partner(0, after)
    products(after, False)
    relay(1)
    hand_over_far(0)
    hand_over(1)
    from_partner(0, across)
    products(across, False)

    arrived(comb.at[1 - xl], crecv)
    for bx in range(N):
        column = comb[bx % 2][:, (bx // 2) * 128 : (bx // 2) * 128 + 128].T
        rows = slice(bx * N * ROWS, (bx + 1) * N * ROWS)
        for w in range(EXPERTS):
            g = acc[w, rows, 0:UNITS]
            u = acc[w, rows, UNITS : 2 * UNITS]
            value = g / (1.0 + jnp.exp(-g)) * u * column[:, w : w + 1]
            hid[rows, w * UNITS : (w + 1) * UNITS] = value.astype(BF16)

    def cols_of(j, cy):
        return pl.ds(pl.multiple_of(cy * QUARTER + (j % 2) * WIDE, 128), WIDE)

    def down_product(j, cy):
        cols = cols_of(j, cy)
        right = jnp.concatenate([ws[6 + w, cols, :] for w in range(EXPERTS)], axis=1)
        total = lax.dot_general(
            hid[...], right, (((1,), (1,)), ((), ())), preferred_element_type=F32
        )
        part[:, :, :, cols] = total.astype(BF16).reshape(N, N, ROWS, WIDE)
        for i, d in enumerate((1, 3, 2)):
            if j % 2 == 0:
                src = part.at[ring(x, d), :, :, cols]
            else:
                src = part.at[:, ring(z, d), :, cols]
            send(src, r1.at[i, :, :, cols], rrecv1.at[j, i], along(j % 2, d))

    def sum_first(j, cy):
        cols = cols_of(j, cy)
        own = part[x, :, :, cols] if j % 2 == 0 else part[:, z, :, cols]
        total = own.astype(F32)
        for i in range(3):
            arrived(r1.at[i, :, :, cols], rrecv1.at[j, i])
            total = total + r1[i, :, :, cols].astype(F32)
        s1[:, :, cols] = total.astype(BF16)
        for i, d in enumerate((1, 3, 2)):
            to = ring(z, d) if j % 2 == 0 else ring(x, d)
            send(s1.at[to, :, cols], r2.at[i, :, cols], rrecv2.at[j, i], along(1 - j % 2, d))

    def sum_second(j, cy):
        cols = cols_of(j, cy)
        total = s1[z if j % 2 == 0 else x, :, cols].astype(F32)
        for i in range(3):
            arrived(r2.at[i, :, cols], rrecv2.at[j, i])
            total = total + r2[i, :, cols].astype(F32)
        out[:, cols] = total.astype(BF16)

    order = [y, y, before, before, after, after, across, across]
    for j in range(PIECES):
        if j % 2 == 0:
            if j == 6:
                hand_over_far(1)
            from_partner(1, order[j])
        down_product(j, order[j])
    for j in range(PIECES):
        sum_first(j, order[j])
    for j in range(PIECES):
        sum_second(j, order[j])

    for cp in sends:
        cp.wait_send()
    arrived(ws.at[0:6, 0 : 15 * DEPTH, :], asend.at[0])
    arrived(ws.at[6:9, 0 : 15 * DEPTH, :], asend.at[1])


SENDS = 1 + 30 + 28 + 48


def local(tokens, expert_ids, gate_scores, gate_weight, up_weight, down_weight):
    any_space = pl.BlockSpec(memory_space=pl.ANY)
    vmem = pl.BlockSpec(memory_space=pltpu.VMEM)
    dma = pltpu.SemaphoreType.DMA
    return pl.pallas_call(
        kernel,
        out_shape=jax.ShapeDtypeStruct((ROWS, D), BF16),
        in_specs=[any_space, vmem, vmem, any_space, any_space, any_space],
        out_specs=vmem,
        scratch_shapes=[
            pltpu.VMEM((N, N, ROWS, D), BF16),
            pltpu.VMEM((3 * EXPERTS, D, UNITS), BF16),
            pltpu.VMEM((EXPERTS, N * N * ROWS, 2 * UNITS), F32),
            pltpu.VMEM((N * N * ROWS, EXPERTS * UNITS), BF16),
            pltpu.VMEM((N, N, ROWS, D), BF16),
            pltpu.VMEM((3, N, ROWS, D), BF16),
            pltpu.VMEM((N, ROWS, D), BF16),
            pltpu.VMEM((3, ROWS, D), BF16),
            pltpu.VMEM((2, 8, 256), F32),
            dma((SENDS,)),
            dma((2,)),
            dma((2, 2)),
            dma((2, 16)),
            dma((2, N, N)),
            dma,
            dma((PIECES, 3)),
            dma((PIECES, 3)),
            dma,
        ],
        compiler_params=pltpu.CompilerParams(
            collective_id=0, has_side_effects=True, vmem_limit_bytes=64000 * 1024
        ),
        name="relay_experts",
    )(tokens, expert_ids.T, gate_scores.T, gate_weight, up_weight, down_weight)


def solution(mesh):
    return jax.shard_map(
        local,
        mesh=mesh,
        in_specs=(
            P(("expert", "tensor"), None),
            P("expert", None),
            P("expert", None),
            P(None, ("expert", "tensor"), None),
            P(None, ("expert", "tensor"), None),
            P(None, ("expert", "tensor"), None),
        ),
        out_specs=P(("expert", "tensor"), None),
        check_vma=False,
    )
```

time: 394 us -> 152 us (0.39)
  waiting for transfers between devices: 262 us -> 0 us
  Pallas kernels: 0 us -> 150 us
  blocking collectives: 53.7 us -> 0 us
  matrix products: 34.1 us -> 0 us
  local copies, waits for them, and re-layouts: 29.2 us -> 1.82 us
  between operations: 13.3 us -> 0.01 us
    all_gather x4 -> x0, waiting for transfers between devices: 180 us -> none  [the longest x1 63.5 us: local(): lax.all_gather(served_gate, 'expert', axis=1, tiled=True)]
    pallas_call x0 -> x1, Pallas kernels: none -> 150 us  [local(): pl.pallas_call(kernel, out_shape=jax.ShapeDtypeStruct((ROWS, D), BF16), i...]
    reduce_scatter x1 -> x0, waiting for transfers between devices: 81.6 us -> none  [local(): lax.psum_scatter(partial_sum.astype(jnp.bfloat16), 'tensor', scatter_dime...]
    all_to_all x3 -> x0, blocking collectives: 53.7 us -> none  [the longest x1 23.3 us: local(): lax.all_to_all(gate_weight, 'tensor', split_axis=2, concat_axis=1, tiled=...]
    dot_general x7 -> x0, matrix products: 34.1 us -> none  [the longest x1 12.5 us: local(): jnp.einsum('etf,edf->td', stacked, lax.all_gather(served_down, 'expert',...]
    unnamed x21 -> x1, local copies, waits for them, and re-layouts: 22.7 us -> 1.82 us
    all_to_all x3 -> x0, local copies, waits for them, and re-layouts: 6.5 us -> none  [the longest x1 2.19 us: local(): lax.all_to_all(up_weight, 'tensor', split_axis=2, concat_axis=1, tiled=True)]
  transfers between devices with their start and end apart: 5 -> 0, of which waited for: 5 -> 0; matrix products, arithmetic and copies ran while one was open for 13% -> 0% of each run, Pallas kernels for 0% -> 0%
where the time goes in v1:
time: 152 us
  Pallas kernels  150 us (99%)
  local copies, waits for them, and re-layouts  1.82 us (1%)
    pallas_call x1, Pallas kernels, local(): pl.pallas_call(kernel, out_shape=jax.ShapeDtypeStruct((ROWS, D), BF16), i...  150 us

profile of v1, /device:TPU:1, one launch (start us, length us, event | category | flops | bytes accessed | tf_op | source)
XLA Modules:
  0.0 151.9 jit_solution(5873433646809014909)
XLA Ops:
  0.0 150.0 %relay_experts.1 = bf16[32,7168]{1,0:T(8,128)(2,1)} custom-call(bf16[32,7168]{1,0:T(8,128)(2,1)} %tok.1, s32[2,256]{1,0:T(2,128)} %bitcast.2, s32[2,256]{1,0:T(2,128)} %bitcast.3, bf16[3,56,2048]{2,1,0:T(8,128)(2,1)} %gate.1, bf16[3,56,2048]{2,1,0:T(8,128)(2,1)} %up.1, bf16[3,56,2048]{2,1,0:T(8,128)(2,1)} %down.1), custom_call_target="tpu_custom_call" | custom-call | tf_op jit(solution)/shard_map/relay_experts/pallas_call | solution.py:307
  150.0 1.8 %copy.8 = bf16[32,7168]{1,0:T(8,128)(2,1)} copy(bf16[32,7168]{1,0:T(8,128)(2,1)} %relay_experts.1) | data formatting | bytes 917504

commit v2 on v1

--- a/solution.py
+++ b/solution.py
@@ -20,6 +20,7 @@
 HALF = D // 2
 PIECES = 8
 WIDE = D // PIECES
+LAG = 2
 
 PLANE = (
     (1, 0), (3, 0), (0, 1), (0, 3), (2, 0), (0, 2), (1, 1), (3, 3),
@@ -48,7 +49,7 @@
 
 def kernel(
     tok, ids, scores, gate, up, down, out,
-    xs, ws, acc, hid, part, r1, s1, r2, comb,
+    xs, ws, acc, hid, part, ra, r1, s1, rb, r2, comb,
     ssem, asend, arecv, wrecv, trecv, crecv, rrecv1, rrecv2, lsem,
 ):
     e, t, y, x, z, c, xl, xh = place()
@@ -110,7 +111,6 @@
             arecv.at[kind, xl],
         ).start()
 
-    h0, h1 = pl.ds(0, HALF), pl.ds(HALF, HALF)
     own_tok = pltpu.make_async_copy(tok, xs.at[x, z], lsem)
     own_tok.start()
     keep(gate, 0, 0)
@@ -126,15 +126,29 @@
             return device(y, ring(x, d), z, c)
         return device(y, x, ring(z, d), c)
 
-    def send_tokens(src, bx, bz, half, axis):
-        cols = (h0, h1)[half]
-        for d in (1, 3, 2):
-            send(src, xs.at[bx, bz, :, cols], trecv.at[half, bx, bz], along(axis, d))
-
-    send_tokens(tok.at[:, h0], x, z, 0, 0)
-    send_tokens(tok.at[:, h1], x, z, 1, 1)
-    send_tokens(tok.at[:, h0], x, z, 0, 1)
-    send_tokens(tok.at[:, h1], x, z, 1, 0)
+    halves = (pl.ds(0, HALF), pl.ds(HALF, HALF))
+    ALL, LOW, HIGH = pl.ds(0, ROWS), pl.ds(0, ROWS // 2), pl.ds(ROWS // 2, ROWS // 2)
+
+    def block(half, a, b):
+        if half == 0:
+            return ring(x, a), ring(z, b)
+        return ring(x, b), ring(z, a)
+
+    def send_tokens(half, leg, a, b, d, rows=ALL, src=None):
+        bx, bz = block(half, a, b)
+        cols = halves[half]
+        dst = xs.at[bx, bz, rows, cols]
+        to = along(leg if half == 0 else 1 - leg, d)
+        send(dst if src is None else src.at[rows, cols], dst, trecv.at[half, bx, bz], to)
+
+    def wait_tokens(half, a, b):
+        bx, bz = block(half, a, b)
+        arrived(xs.at[bx, bz, :, halves[half]], trecv.at[half, bx, bz])
+
+    for leg in range(2):
+        for half in range(2):
+            for d in (1, 3):
+                send_tokens(half, leg, 0, 0, d, src=tok)
     spread(down, 6, 1)
 
     bounds = ((0, 6), (6, 9))
@@ -188,25 +202,42 @@
         for cx in range(2):
             wait_chunk(kind, cy, cx, 1 - c)
 
-    def wait_tokens(bx, bz, half):
-        arrived(xs.at[bx, bz, :, (h0, h1)[half]], trecv.at[half, bx, bz])
+    def second_leg(half, a):
+        send_tokens(half, 1, a, 0, 1)
+        send_tokens(half, 1, a, 0, 3)
+
+    def second_relay(half, a):
+        wait_tokens(half, a, 3)
+        if a in (0, 3):
+            send_tokens(half, 1, a, 3, 1)
+        wait_tokens(half, a, 1)
+        if a in (1, 2):
+            send_tokens(half, 1, a, 1, 3)
 
     own_chunks(0)
-    for d in (3, 1, 2):
-        bx = ring(x, d)
-        wait_tokens(bx, z, 0)
-        send_tokens(xs.at[bx, z, :, h0], bx, z, 0, 1)
-        bz = ring(z, d)
-        wait_tokens(x, bz, 1)
-        send_tokens(xs.at[x, bz, :, h1], x, bz, 1, 0)
+    for half in range(2):
+        wait_tokens(half, 3, 0)
+        send_tokens(half, 0, 3, 0, 1, LOW)
+        second_leg(half, 3)
+    for half in range(2):
+        wait_tokens(half, 1, 0)
+        send_tokens(half, 0, 1, 0, 3, HIGH)
+        second_leg(half, 1)
+    for half in range(2):
+        second_relay(half, 0)
+    for half in range(2):
+        wait_tokens(half, 2, 0)
+        second_leg(half, 2)
     relay(0)
     own_chunks(1)
+    for a in (3, 1, 2):
+        for half in range(2):
+            second_relay(half, a)
     hand_over(0)
     own_tok.wait()
-    for bd in range(1, N):
-        for ad in range(N):
-            wait_tokens(ring(x, ad), ring(z, bd), 0)
-            wait_tokens(ring(x, bd), ring(z, ad), 1)
+    for a in range(N):
+        for half in range(2):
+            wait_tokens(half, a, 2)
 
     def products(cy, start):
         span = pl.ds(pl.multiple_of(cy * QUARTER, 256), QUARTER)
@@ -252,44 +283,84 @@
             hid[...], right, (((1,), (1,)), ((), ())), preferred_element_type=F32
         )
         part[:, :, :, cols] = total.astype(BF16).reshape(N, N, ROWS, WIDE)
-        for i, d in enumerate((1, 3, 2)):
-            if j % 2 == 0:
-                src = part.at[ring(x, d), :, :, cols]
-            else:
-                src = part.at[:, ring(z, d), :, cols]
-            send(src, r1.at[i, :, :, cols], rrecv1.at[j, i], along(j % 2, d))
-
-    def sum_first(j, cy):
-        cols = cols_of(j, cy)
-        own = part[x, :, :, cols] if j % 2 == 0 else part[:, z, :, cols]
+
+    def add_into(ref, more):
+        ref[...] = (ref[...].astype(F32) + more[...].astype(F32)).astype(BF16)
+
+    def share(axis, b, half, cols):
+        if axis == 0:
+            return part.at[b, 2 * half : 2 * half + 2, :, cols]
+        return part.at[2 * half : 2 * half + 2, b, :, cols]
+
+    def first_send(j, cy):
+        down_product(j, cy)
+        cols, axis = cols_of(j, cy), j % 2
+        me = (x, z)[axis]
+        sem = lambda i: rrecv1.at[j, i]
+        far = ring(me, 2)
+        send(share(axis, far, 0, cols), ra.at[0, :, :, cols], sem(0), along(axis, 1))
+        send(share(axis, far, 1, cols), ra.at[1, :, :, cols], sem(1), along(axis, 3))
+        send(share(axis, ring(me, 1), 1, cols), r1.at[0, 2:4, :, cols], sem(2), along(axis, 1))
+        send(share(axis, ring(me, 3), 0, cols), r1.at[1, 0:2, :, cols], sem(3), along(axis, 3))
+
+    def first_relay(j, cy):
+        cols, axis = cols_of(j, cy), j % 2
+        me = (x, z)[axis]
+        for i, d in enumerate((1, 3)):
+            more = ra.at[i, :, :, cols]
+            arrived(more, rrecv1.at[j, i])
+            ref = share(axis, ring(me, d), i, cols)
+            add_into(ref, more)
+            send(ref, r1.at[i, 2 * i : 2 * i + 2, :, cols], rrecv1.at[j, 4 + i], along(axis, d))
+
+    def first_sum(j, cy):
+        cols, axis = cols_of(j, cy), j % 2
+        own = part[x, :, :, cols] if axis == 0 else part[:, z, :, cols]
         total = own.astype(F32)
-        for i in range(3):
-            arrived(r1.at[i, :, :, cols], rrecv1.at[j, i])
+        for i in range(2):
+            arrived(r1.at[i, 2 - 2 * i : 4 - 2 * i, :, cols], rrecv1.at[j, 2 + i])
+            arrived(r1.at[i, 2 * i : 2 * i + 2, :, cols], rrecv1.at[j, 4 + i])
             total = total + r1[i, :, :, cols].astype(F32)
         s1[:, :, cols] = total.astype(BF16)
-        for i, d in enumerate((1, 3, 2)):
-            to = ring(z, d) if j % 2 == 0 else ring(x, d)
-            send(s1.at[to, :, cols], r2.at[i, :, cols], rrecv2.at[j, i], along(1 - j % 2, d))
-
-    def sum_second(j, cy):
-        cols = cols_of(j, cy)
-        total = s1[z if j % 2 == 0 else x, :, cols].astype(F32)
-        for i in range(3):
-            arrived(r2.at[i, :, cols], rrecv2.at[j, i])
+        me, axis = (z, x)[axis], 1 - axis
+        far = ring(me, 2)
+        sem = lambda i: rrecv2.at[j, i]
+        send(s1.at[far, LOW, cols], rb.at[0, :, cols], sem(0), along(axis, 1))
+        send(s1.at[far, HIGH, cols], rb.at[1, :, cols], sem(1), along(axis, 3))
+        send(s1.at[ring(me, 1), HIGH, cols], r2.at[0, HIGH, cols], sem(2), along(axis, 1))
+        send(s1.at[ring(me, 3), LOW, cols], r2.at[1, LOW, cols], sem(3), along(axis, 3))
+
+    def second_relay_sum(j, cy):
+        cols, axis = cols_of(j, cy), 1 - j % 2
+        me = (x, z)[axis]
+        for i, d in enumerate((1, 3)):
+            rows = (LOW, HIGH)[i]
+            more = rb.at[i, :, cols]
+            arrived(more, rrecv2.at[j, i])
+            ref = s1.at[ring(me, d), rows, cols]
+            add_into(ref, more)
+            send(ref, r2.at[i, rows, cols], rrecv2.at[j, 4 + i], along(axis, d))
+
+    def second_sum(j, cy):
+        cols, axis = cols_of(j, cy), 1 - j % 2
+        total = s1[(x, z)[axis], :, cols].astype(F32)
+        for i in range(2):
+            arrived(r2.at[i, (HIGH, LOW)[i], cols], rrecv2.at[j, 2 + i])
+            arrived(r2.at[i, (LOW, HIGH)[i], cols], rrecv2.at[j, 4 + i])
             total = total + r2[i, :, cols].astype(F32)
         out[:, cols] = total.astype(BF16)
 
     order = [y, y, before, before, after, after, across, across]
-    for j in range(PIECES):
-        if j % 2 == 0:
-            if j == 6:
+    stages = (first_send, first_relay, first_sum, second_relay_sum, second_sum)
+    for n in range(PIECES + LAG * (len(stages) - 1)):
+        if n < PIECES and n % 2 == 0:
+            if n == 6:
                 hand_over_far(1)
-            from_partner(1, order[j])
-        down_product(j, order[j])
-    for j in range(PIECES):
-        sum_first(j, order[j])
-    for j in range(PIECES):
-        sum_second(j, order[j])
+            from_partner(1, order[n])
+        for i, stage in enumerate(stages):
+            j = n - LAG * i
+            if 0 <= j < PIECES:
+                stage(j, order[j])
 
     for cp in sends:
         cp.wait_send()
@@ -297,7 +368,7 @@
     arrived(ws.at[6:9, 0 : 15 * DEPTH, :], asend.at[1])
 
 
-SENDS = 1 + 30 + 28 + 48
+SENDS = 1 + 16 + 4 + 12 + 4 + 28 + 96 + 8
 
 
 def local(tokens, expert_ids, gate_scores, gate_weight, up_weight, down_weight):
@@ -315,9 +386,11 @@
             pltpu.VMEM((EXPERTS, N * N * ROWS, 2 * UNITS), F32),
             pltpu.VMEM((N * N * ROWS, EXPERTS * UNITS), BF16),
             pltpu.VMEM((N, N, ROWS, D), BF16),
-            pltpu.VMEM((3, N, ROWS, D), BF16),
+            pltpu.VMEM((2, N // 2, ROWS, D), BF16),
+            pltpu.VMEM((2, N, ROWS, D), BF16),
             pltpu.VMEM((N, ROWS, D), BF16),
-            pltpu.VMEM((3, ROWS, D), BF16),
+            pltpu.VMEM((2, ROWS // 2, D), BF16),
+            pltpu.VMEM((2, ROWS, D), BF16),
             pltpu.VMEM((2, 8, 256), F32),
             dma((SENDS,)),
             dma((2,)),
@@ -325,8 +398,8 @@
             dma((2, 16)),
             dma((2, N, N)),
             dma,
-            dma((PIECES, 3)),
-            dma((PIECES, 3)),
+            dma((PIECES, 6)),
+            dma((PIECES, 6)),
             dma,
         ],
         compiler_params=pltpu.CompilerParams(

time: 152 us -> 142 us (0.934)
  Pallas kernels: 150 us -> 139 us
    pallas_call x1, Pallas kernels: 150 us -> 139 us  [local(): pl.pallas_call(kernel, out_shape=jax.ShapeDtypeStruct((ROWS, D), BF16), i...]
where the time goes in v2:
time: 142 us; the launch traced here: 141 us
  Pallas kernels  139 us (98%)
  local copies, waits for them, and re-layouts  1.82 us (1%)
    pallas_call x1, Pallas kernels, local(): pl.pallas_call(kernel, out_shape=jax.ShapeDtypeStruct((ROWS, D), BF16), i...  139 us

profile of v2, /device:TPU:1, one launch (start us, length us, event | category | flops | bytes accessed | tf_op | source)
XLA Modules:
  0.0 140.7 jit_solution(5698005483983522088)
XLA Ops:
  0.0 138.9 %relay_experts.1 = bf16[32,7168]{1,0:T(8,128)(2,1)} custom-call(bf16[32,7168]{1,0:T(8,128)(2,1)} %tok.1, s32[2,256]{1,0:T(2,128)} %bitcast.2, s32[2,256]{1,0:T(2,128)} %bitcast.3, bf16[3,56,2048]{2,1,0:T(8,128)(2,1)} %gate.1, bf16[3,56,2048]{2,1,0:T(8,128)(2,1)} %up.1, bf16[3,56,2048]{2,1,0:T(8,128)(2,1)} %down.1), custom_call_target="tpu_custom_call" | custom-call | tf_op jit(solution)/shard_map/relay_experts/pallas_call | solution.py:378
  138.9 1.8 %copy.8 = bf16[32,7168]{1,0:T(8,128)(2,1)} copy(bf16[32,7168]{1,0:T(8,128)(2,1)} %relay_experts.1) | data formatting | bytes 917504

commit v3 on v0

v3 whole, which is shorter than its diff:
```python
import jax
import jax.numpy as jnp
from jax import lax
from jax.experimental import pallas as pl
from jax.experimental.pallas import tpu as pltpu
from jax.sharding import PartitionSpec as P

MESH = pl.DeviceIdType.MESH
F32 = jnp.float32
BF16 = jnp.bfloat16

N = 4
EXPERTS = 3
D = 7168
FF = 2048
ROWS = 32
GROUP = N * N * ROWS
DEPTH = 56
CHUNK = 448
QUARTER = 1792
UNITS = 128
SPAN = 896

PLANE = (
    (1, 0), (3, 0), (0, 1), (0, 3), (2, 0), (0, 2), (1, 1), (3, 3),
    (2, 1), (1, 3), (3, 1), (2, 3), (1, 2), (3, 2), (2, 2),
)


def place():
    e = lax.axis_index("expert")
    t = lax.axis_index("tensor")
    y, xl, c = lax.div(e, 4), lax.rem(lax.div(e, 2), 2), lax.rem(e, 2)
    xh, z = lax.div(t, 4), lax.rem(t, 4)
    return e, t, y, xh * 2 + xl, z, c, xl, xh


def device(y, x, z, c):
    return {
        "expert": y * 4 + lax.rem(x, 2) * 2 + c,
        "tensor": lax.div(x, 2) * 4 + z,
    }


def ring(v, d):
    return lax.rem(v + d, N)


def kernel(
    tok, ids, scores, gate, up, down, out,
    xs, wg, wd, acc, hb, mask, total_ref, ob, back, order_ref, info,
    ssem, asend, arecv, wrecv, drecv, trecv, hrecv, irecv, osem, lsem,
):
    e_index, t_index, y, x, z, c, xl, xh = place()
    mine = e_index * 8 + t_index
    sends = []

    def send(src, dst, recv, to):
        cp = pltpu.make_async_remote_copy(
            src_ref=src,
            dst_ref=dst,
            send_sem=ssem.at[len(sends)],
            recv_sem=recv,
            device_id=to,
            device_id_type=MESH,
        )
        cp.start()
        sends.append(cp)

    def arrived(ref, sem):
        pltpu.make_async_copy(ref, ref, sem).wait()

    barrier = pltpu.get_barrier_semaphore()
    peers = [device(y, ring(x, dx), ring(z, dz), c) for dx, dz in PLANE]
    north, south = device(ring(y, 1), x, z, c), device(ring(y, 3), x, z, c)
    partner = device(y, x, z, 1 - c)
    for to in [*peers, north, south, partner]:
        pl.semaphore_signal(barrier, inc=1, device_id=to, device_id_type=MESH)

    marks = scores[...].astype(F32)
    info[xl, 0:2, :] = ids[...].astype(F32)
    info[xl, 2:4, :] = marks / (marks[0:1, :] + marks[1:2, :])

    own_rows = pl.ds(pl.multiple_of(mine * DEPTH, 8), DEPTH)
    before, after, across = ring(y, 3), ring(y, 1), ring(y, 2)

    def columns(px, pz):
        return pl.ds(pl.multiple_of((px * N + pz) * UNITS, UNITS), UNITS)

    own_tok = pltpu.make_async_copy(tok, xs.at[x, z], lsem)
    own_tok.start()
    for w in range(EXPERTS):
        for i, ref in enumerate((gate, up)):
            pltpu.make_async_copy(
                ref.at[w, :, columns(x, z)], wg.at[2 * w + i, own_rows, :], arecv.at[w, xl]
            ).start()

    def down_piece(w, cy, cc, cols=slice(None)):
        rows = pl.ds(pl.multiple_of(cc * DEPTH, 8), DEPTH)
        return wd.at[w, cy, rows, cols]

    own_down = []
    for w in range(EXPERTS):
        cp = pltpu.make_async_copy(down.at[w], down_piece(w, y, c), drecv.at[w, y, c])
        cp.start()
        own_down.append(cp)

    pl.semaphore_wait(barrier, len(peers) + 3)

    def down_own(w):
        for to in (north, south, partner):
            send(down.at[w], down_piece(w, y, c), drecv.at[w, y, c], to)

    def down_pass(w, cy, to, cols=slice(None)):
        ref = down_piece(w, cy, c, cols)
        send(ref, ref, drecv.at[w, cy, c], to)

    def down_wait(w, cy, cc):
        arrived(down_piece(w, cy, cc), drecv.at[w, cy, cc])

    def down_relay(w):
        down_wait(w, before, c)
        down_pass(w, before, north, slice(0, FF // 2))
        down_wait(w, after, c)
        down_pass(w, after, south, slice(FF // 2, FF))
        down_pass(w, before, partner)
        down_pass(w, after, partner)

    def down_far(w):
        down_wait(w, across, c)
        down_pass(w, across, partner)

    def spread(w):
        for (dx, dz), to in zip(PLANE, peers):
            cols = columns(ring(x, dx), ring(z, dz))
            for i, ref in enumerate((gate, up)):
                pltpu.make_async_remote_copy(
                    src_ref=ref.at[w, :, cols],
                    dst_ref=wg.at[2 * w + i, own_rows, :],
                    send_sem=asend.at[w],
                    recv_sem=arecv.at[w, xl],
                    device_id=to,
                    device_id_type=MESH,
                ).start()

    def chunk(w, cy, cx, cc):
        k = cy * 4 + cx * 2 + cc
        rows = pl.ds(pl.multiple_of(k * CHUNK, CHUNK), CHUNK)
        return wg.at[2 * w : 2 * w + 2, rows, :], wrecv.at[w, k]

    def pass_on(w, cy, cx, to):
        ref, sem = chunk(w, cy, cx, c)
        send(ref, ref, sem, to)

    def wait_chunk(w, cy, cx, cc):
        ref, sem = chunk(w, cy, cx, cc)
        arrived(ref, sem)

    def own_chunks(w):
        arrived(chunk(w, y, 0, c)[0], arecv.at[w, 0])
        pass_on(w, y, 0, north)
        arrived(chunk(w, y, 1, c)[0], arecv.at[w, 1])
        pass_on(w, y, 1, south)
        pass_on(w, y, 1, north)
        pass_on(w, y, 0, south)
        pass_on(w, y, 0, partner)
        pass_on(w, y, 1, partner)

    def relay(w):
        wait_chunk(w, before, 0, c)
        pass_on(w, before, 0, north)
        wait_chunk(w, after, 1, c)
        pass_on(w, after, 1, south)
        pass_on(w, before, 0, partner)
        pass_on(w, after, 1, partner)

    def hand_over(w):
        wait_chunk(w, before, 1, c)
        pass_on(w, before, 1, partner)
        wait_chunk(w, after, 0, c)
        pass_on(w, after, 0, partner)

    def hand_over_far(w):
        for cx in range(2):
            wait_chunk(w, across, cx, c)
            pass_on(w, across, cx, partner)

    def from_partner(w):
        for cy in (y, before, after, across):
            for cx in range(2):
                wait_chunk(w, cy, cx, 1 - c)

    class Gather:
        def __init__(self, ref, sem, whole, low, high):
            self.ref, self.sem, self.whole, self.low, self.high = ref, sem, whole, low, high

        def block(self, half, a, b):
            return (ring(x, a), ring(z, b)) if half == 0 else (ring(x, b), ring(z, a))

        def to(self, half, leg, d):
            if (half + leg) % 2 == 0:
                return device(y, ring(x, d), z, c)
            return device(y, x, ring(z, d), c)

        def send(self, half, leg, a, b, d, part=None, src=None):
            bx, bz = self.block(half, a, b)
            part = (part or self.whole)[half]
            dst = self.ref.at[bx, bz, part[0], part[1]]
            src = dst if src is None else src.at[part[0], part[1]]
            send(src, dst, self.sem.at[half, bx, bz], self.to(half, leg, d))

        def wait(self, half, a, b):
            bx, bz = self.block(half, a, b)
            part = self.whole[half]
            arrived(self.ref.at[bx, bz, part[0], part[1]], self.sem.at[half, bx, bz])

        def start(self, src=None):
            for leg in range(2):
                for half in range(2):
                    for d in (1, 3):
                        self.send(half, leg, 0, 0, d, src=src)

        def near(self, a):
            for half in range(2):
                self.wait(half, a, 0)
                if a == 3:
                    self.send(half, 0, 3, 0, 1, self.low)
                elif a == 1:
                    self.send(half, 0, 1, 0, 3, self.high)
                self.send(half, 1, a, 0, 1)
                self.send(half, 1, a, 0, 3)

        def relay(self, a):
            for half in range(2):
                self.wait(half, a, 3)
                if a in (0, 3):
                    self.send(half, 1, a, 3, 1)
                self.wait(half, a, 1)
                if a in (1, 2):
                    self.send(half, 1, a, 1, 3)

        def far(self, a):
            for half in range(2):
                self.wait(half, a, 2)

    rows_all = pl.ds(0, ROWS)
    sides = (pl.ds(0, D // 2), pl.ds(D // 2, D // 2))
    upper, lower = pl.ds(0, ROWS // 2), pl.ds(ROWS // 2, ROWS // 2)
    tokens = Gather(
        xs, trecv,
        [(rows_all, s) for s in sides],
        [(upper, s) for s in sides],
        [(lower, s) for s in sides],
    )
    every = pl.ds(0, 2 * UNITS)
    fourths = [pl.ds(i * GROUP // 4, GROUP // 4) for i in range(4)]
    hidden = Gather(
        hb, hrecv,
        [(pl.ds(i * GROUP // 2, GROUP // 2), every) for i in range(2)],
        [(fourths[0], every), (fourths[2], every)],
        [(fourths[1], every), (fourths[3], every)],
    )

    down_own(0)
    spread(0)
    spread(1)
    send(info.at[xl], info.at[xl], irecv, device(y, xh * 2 + 1 - xl, z, c))
    tokens.start(tok)
    spread(2)

    wd[:, :, 2 * DEPTH :, :] = jnp.zeros((EXPERTS, N, 128 - 2 * DEPTH, FF), BF16)
    lane = lax.broadcasted_iota(jnp.int32, (128, SPAN), 0)
    wanted = lax.broadcasted_iota(jnp.int32, (128, SPAN), 1)
    for q in range(8):
        spot = jnp.where(lane < DEPTH, lane, lane + CHUNK - DEPTH) + q * DEPTH
        spot = jnp.where(lane < 2 * DEPTH, spot, -1)
        order_ref[q * 128 : (q + 1) * 128, :] = jnp.where(spot == wanted, 1.0, 0.0).astype(BF16)

    arrived(info.at[1 - xl], irecv)
    route = []
    for bx in range(N):
        column = info[bx % 2][:, (bx // 2) * 128 : (bx // 2) * 128 + 128].T
        route.append(column)
        rows = slice(bx * N * ROWS, (bx + 1) * N * ROWS)
        for k in range(2):
            for w in range(EXPERTS):
                hit = jnp.where(column[:, k : k + 1] == float(w), 1.0, 0.0)
                mask[k, w, rows, :] = jnp.broadcast_to(hit, (N * ROWS, UNITS)).astype(BF16)

    own_chunks(0)
    own_chunks(1)
    relay(0)
    tokens.near(3)
    tokens.near(1)
    tokens.relay(0)
    hand_over(0)
    own_chunks(2)
    tokens.near(2)
    relay(1)
    hand_over_far(0)
    down_own(1)
    down_own(2)
    tokens.relay(3)
    tokens.relay(1)
    hand_over(1)
    relay(2)
    tokens.relay(2)
    down_relay(0)
    own_tok.wait()
    for a in range(N):
        tokens.far(a)

    def products(w):
        def one(q, carry):
            span = pl.ds(pl.multiple_of(q * QUARTER, 256), QUARTER)
            left = xs[:, :, :, span].reshape(GROUP, QUARTER)
            right = jnp.concatenate([wg[2 * w, span, :], wg[2 * w + 1, span, :]], axis=1)
            acc[w] += jnp.dot(left, right, preferred_element_type=F32)
            return carry

        acc[w] = jnp.zeros((GROUP, 2 * UNITS), F32)
        lax.fori_loop(0, N, one, 0)

    from_partner(0)
    products(0)
    hand_over_far(1)
    from_partner(1)
    products(1)
    hand_over(2)
    hand_over_far(2)
    from_partner(2)
    products(2)

    for bx in range(N):
        rows = slice(bx * N * ROWS, (bx + 1) * N * ROWS)
        values = []
        for w in range(EXPERTS):
            g = acc[w, rows, 0:UNITS]
            u = acc[w, rows, UNITS : 2 * UNITS]
            values.append(g / (1.0 + jnp.exp(-g)) * u)
        column = info[bx % 2][:, (bx // 2) * 128 : (bx // 2) * 128 + 128].T
        for k in range(2):
            chosen = column[:, k : k + 1]
            value = jnp.where(chosen == 0.0, values[0], jnp.where(chosen == 1.0, values[1], values[2]))
            value = value * column[:, 2 + k : 3 + k]
            hb[x, z, rows, k * UNITS : (k + 1) * UNITS] = value.astype(BF16)

    def down_products(half, a):
        rows = pl.ds(half * GROUP // 2, GROUP // 2)
        left, right = [], []
        for b in range(N):
            bx, bz = hidden.block(half, a, b)
            one, two = hb[bx, bz, rows, 0:UNITS], hb[bx, bz, rows, UNITS : 2 * UNITS]
            for w in range(EXPERTS):
                left.append(one * mask[0, w, rows, :] + two * mask[1, w, rows, :])
                right.append(wd[w, :, :, columns(bx, bz)].reshape(N * 128, UNITS))
        more = lax.dot_general(
            jnp.concatenate(left, axis=1), jnp.concatenate(right, axis=1),
            (((1,), (1,)), ((), ())), preferred_element_type=F32,
        )
        total_ref[rows, :] = more if a == 0 else total_ref[rows, :] + more

    hidden.start()
    down_relay(1)
    hidden.near(3)
    hidden.near(1)
    hidden.relay(0)
    down_relay(2)
    hidden.near(2)
    for w in range(EXPERTS):
        down_far(w)
    hidden.relay(3)
    hidden.relay(1)
    hidden.relay(2)
    for w in range(EXPERTS):
        own_down[w].wait()
        for cy in (y, before, after, across):
            down_wait(w, cy, 1 - c)
    for a in (0, 3, 1, 2):
        hidden.far(a)
        for half in range(2):
            down_products(half, a)

    for cy in range(N):
        piece = total_ref[:, cy * 128 : (cy + 1) * 128].astype(BF16)
        ob[:, :, cy, :, :] = piece.reshape(N, N, ROWS, 128)
    spot = back.at[xl, :, :, pl.ds(pl.multiple_of(t_index * 128, 128), 128)]
    for (dx, dz), to in zip(PLANE, peers):
        send(ob.at[ring(x, dx), ring(z, dz)], spot, osem, to)
    pltpu.make_async_copy(ob.at[x, z], spot, osem).start()
    arrived(back, osem)
    result = jnp.dot(
        back[...].reshape(2 * N * ROWS, 8 * 128), order_ref[...], preferred_element_type=F32
    ).astype(BF16)
    for cx in range(2):
        for cy in range(N):
            k = cx * N + cy
            base = (cy * 2 + cx) * SPAN
            out[:, base : base + SPAN] = result[k * ROWS : (k + 1) * ROWS, :]

    for cp in sends:
        cp.wait_send()
    for w in range(EXPERTS):
        arrived(wg.at[0:2, 0 : 15 * DEPTH, :], asend.at[w])


SENDS = 146


def local(tokens, expert_ids, gate_scores, gate_weight, up_weight, down_weight):
    any_space = pl.BlockSpec(memory_space=pl.ANY)
    vmem = pl.BlockSpec(memory_space=pltpu.VMEM)
    dma = pltpu.SemaphoreType.DMA
    return pl.pallas_call(
        kernel,
        out_shape=jax.ShapeDtypeStruct((ROWS, D), BF16),
        in_specs=[any_space, vmem, vmem, any_space, any_space, any_space],
        out_specs=vmem,
        scratch_shapes=[
            pltpu.VMEM((N, N, ROWS, D), BF16),
            pltpu.VMEM((2 * EXPERTS, D, UNITS), BF16),
            pltpu.VMEM((EXPERTS, N, 128, FF), BF16),
            pltpu.VMEM((EXPERTS, GROUP, 2 * UNITS), F32),
            pltpu.VMEM((N, N, GROUP, 2 * UNITS), BF16),
            pltpu.VMEM((2, EXPERTS, GROUP, UNITS), BF16),
            pltpu.VMEM((GROUP, N * 128), F32),
            pltpu.VMEM((N, N, N, ROWS, 128), BF16),
            pltpu.VMEM((2, N, ROWS, 8 * 128), BF16),
            pltpu.VMEM((8 * 128, SPAN), BF16),
            pltpu.VMEM((2, 8, 256), F32),
            dma((SENDS,)),
            dma((EXPERTS,)),
            dma((EXPERTS, 2)),
            dma((EXPERTS, 16)),
            dma((EXPERTS, N, 2)),
            dma((2, N, N)),
            dma((2, N, N)),
            dma,
            dma,
            dma,
        ],
        compiler_params=pltpu.CompilerParams(
            collective_id=0, has_side_effects=True, vmem_limit_bytes=64000 * 1024
        ),
        name="relay_experts",
    )(tokens, expert_ids.T, gate_scores.T, gate_weight, up_weight, down_weight)


def solution(mesh):
    return jax.shard_map(
        local,
        mesh=mesh,
        in_specs=(
            P(("expert", "tensor"), None),
            P("expert", None),
            P("expert", None),
            P(None, ("expert", "tensor"), None),
            P(None, ("expert", "tensor"), None),
            P(None, ("expert", "tensor"), None),
        ),
        out_specs=P(("expert", "tensor"), None),
        check_vma=False,
    )
```

time: 394 us -> 125 us (0.32)
  waiting for transfers between devices: 262 us -> 0 us
  Pallas kernels: 0 us -> 123 us
  blocking collectives: 53.7 us -> 0 us
  matrix products: 34.1 us -> 0 us
  local copies, waits for them, and re-layouts: 29.2 us -> 1.82 us
  between operations: 13.3 us -> 0.01 us
    all_gather x4 -> x0, waiting for transfers between devices: 180 us -> none  [the longest x1 63.5 us: local(): lax.all_gather(served_gate, 'expert', axis=1, tiled=True)]
    pallas_call x0 -> x1, Pallas kernels: none -> 123 us  [local(): pl.pallas_call(kernel, out_shape=jax.ShapeDtypeStruct((ROWS, D), BF16), i...]
    reduce_scatter x1 -> x0, waiting for transfers between devices: 81.6 us -> none  [local(): lax.psum_scatter(partial_sum.astype(jnp.bfloat16), 'tensor', scatter_dime...]
    all_to_all x3 -> x0, blocking collectives: 53.7 us -> none  [the longest x1 23.3 us: local(): lax.all_to_all(gate_weight, 'tensor', split_axis=2, concat_axis=1, tiled=...]
    dot_general x7 -> x0, matrix products: 34.1 us -> none  [the longest x1 12.5 us: local(): jnp.einsum('etf,edf->td', stacked, lax.all_gather(served_down, 'expert',...]
    unnamed x21 -> x1, local copies, waits for them, and re-layouts: 22.7 us -> 1.82 us
    all_to_all x3 -> x0, local copies, waits for them, and re-layouts: 6.5 us -> none  [the longest x1 2.19 us: local(): lax.all_to_all(up_weight, 'tensor', split_axis=2, concat_axis=1, tiled=True)]
  transfers between devices with their start and end apart: 5 -> 0, of which waited for: 5 -> 0; matrix products, arithmetic and copies ran while one was open for 13% -> 0% of each run, Pallas kernels for 0% -> 0%
where the time goes in v3:
time: 125 us; the launch traced here: 124 us
  Pallas kernels  123 us (98%)
  local copies, waits for them, and re-layouts  1.82 us (1%)
    pallas_call x1, Pallas kernels, local(): pl.pallas_call(kernel, out_shape=jax.ShapeDtypeStruct((ROWS, D), BF16), i...  123 us

profile of v3, /device:TPU:1, one launch (start us, length us, event | category | flops | bytes accessed | tf_op | source)
XLA Modules:
  0.0 124.5 jit_solution(17345207654825764118)
XLA Ops:
  0.0 122.7 %relay_experts.1 = bf16[32,7168]{1,0:T(8,128)(2,1)} custom-call(bf16[32,7168]{1,0:T(8,128)(2,1)} %tok.1, s32[2,256]{1,0:T(2,128)} %bitcast.2, s32[2,256]{1,0:T(2,128)} %bitcast.3, bf16[3,56,2048]{2,1,0:T(8,128)(2,1)} %gate.1, bf16[3,56,2048]{2,1,0:T(8,128)(2,1)} %up.1, bf16[3,56,2048]{2,1,0:T(8,128)(2,1)} %down.1), custom_call_target="tpu_custom_call" | custom-call | tf_op jit(solution)/shard_map/relay_experts/pallas_call | solution.py:414
  122.7 1.8 %copy.8 = bf16[32,7168]{1,0:T(8,128)(2,1)} copy(bf16[32,7168]{1,0:T(8,128)(2,1)} %relay_experts.1) | data formatting | bytes 917504

commit v4 on v3

--- a/solution.py
+++ b/solution.py
@@ -49,7 +49,7 @@
 def kernel(
     tok, ids, scores, gate, up, down, out,
     xs, wg, wd, acc, hb, mask, total_ref, ob, back, order_ref, info,
-    ssem, asend, arecv, wrecv, drecv, trecv, hrecv, irecv, osem, lsem,
+    ssem, asend, arecv, wrecv, drecv, trecv, hrecv, irecv, osem, fsem, lsem,
 ):
     e_index, t_index, y, x, z, c, xl, xh = place()
     mine = e_index * 8 + t_index
@@ -146,7 +146,7 @@
     def chunk(w, cy, cx, cc):
         k = cy * 4 + cx * 2 + cc
         rows = pl.ds(pl.multiple_of(k * CHUNK, CHUNK), CHUNK)
-        return wg.at[2 * w : 2 * w + 2, rows, :], wrecv.at[w, k]
+        return wg.at[pl.ds(2 * w, 2), rows, :], wrecv.at[w, k]
 
     def pass_on(w, cy, cx, to):
         ref, sem = chunk(w, cy, cx, c)
@@ -185,10 +185,9 @@
             wait_chunk(w, across, cx, c)
             pass_on(w, across, cx, partner)
 
-    def from_partner(w):
-        for cy in (y, before, after, across):
-            for cx in range(2):
-                wait_chunk(w, cy, cx, 1 - c)
+    def from_partner(w, cy):
+        for cx in range(2):
+            wait_chunk(w, cy, cx, 1 - c)
 
     class Gather:
         def __init__(self, ref, sem, whole, low, high):
@@ -244,29 +243,35 @@
                 self.wait(half, a, 2)
 
     rows_all = pl.ds(0, ROWS)
-    sides = (pl.ds(0, D // 2), pl.ds(D // 2, D // 2))
     upper, lower = pl.ds(0, ROWS // 2), pl.ds(ROWS // 2, ROWS // 2)
-    tokens = Gather(
-        xs, trecv,
-        [(rows_all, s) for s in sides],
-        [(upper, s) for s in sides],
-        [(lower, s) for s in sides],
-    )
+
+    def token_gather(i):
+        sides = [pl.ds((2 * i + j) * QUARTER, QUARTER) for j in range(2)]
+        return Gather(
+            xs, trecv.at[i],
+            [(rows_all, s) for s in sides],
+            [(upper, s) for s in sides],
+            [(lower, s) for s in sides],
+        )
+
     every = pl.ds(0, 2 * UNITS)
-    fourths = [pl.ds(i * GROUP // 4, GROUP // 4) for i in range(4)]
-    hidden = Gather(
-        hb, hrecv,
-        [(pl.ds(i * GROUP // 2, GROUP // 2), every) for i in range(2)],
-        [(fourths[0], every), (fourths[2], every)],
-        [(fourths[1], every), (fourths[3], every)],
-    )
+
+    def hidden_gather(i):
+        part = lambda lo, n: pl.ds(i * GROUP // 2 + lo, n)
+        return Gather(
+            hb, hrecv.at[i],
+            [(part(0, 128), every), (part(128, 128), every)],
+            [(part(0, 64), every), (part(128, 64), every)],
+            [(part(64, 64), every), (part(192, 64), every)],
+        )
+
+    tok_a, tok_b = token_gather(0), token_gather(1)
+    hid_a, hid_b = hidden_gather(0), hidden_gather(1)
 
     down_own(0)
     spread(0)
-    spread(1)
     send(info.at[xl], info.at[xl], irecv, device(y, xh * 2 + 1 - xl, z, c))
-    tokens.start(tok)
-    spread(2)
+    tok_a.start(tok)
 
     wd[:, :, 2 * DEPTH :, :] = jnp.zeros((EXPERTS, N, 128 - 2 * DEPTH, FF), BF16)
     lane = lax.broadcasted_iota(jnp.int32, (128, SPAN), 0)
@@ -287,49 +292,77 @@
                 hit = jnp.where(column[:, k : k + 1] == float(w), 1.0, 0.0)
                 mask[k, w, rows, :] = jnp.broadcast_to(hit, (N * ROWS, UNITS)).astype(BF16)
 
+    def quarter(w, q):
+        span = pl.ds(pl.multiple_of(q * QUARTER, 256), QUARTER)
+        left = xs[:, :, :, span].reshape(GROUP, QUARTER)
+        right = jnp.concatenate([wg[2 * w, span, :], wg[2 * w + 1, span, :]], axis=1)
+        acc[w] += jnp.dot(left, right, preferred_element_type=F32)
+
+    def products(w, first):
+        def one(q, carry):
+            quarter(w, q)
+            return carry
+
+        lax.fori_loop(first, first + 2, one, 0)
+
+    def all_from_partner(w):
+        for cy in (y, before, after, across):
+            from_partner(w, cy)
+
+    def tokens_a_here():
+        for a in range(N):
+            tok_a.far(a)
+        own_tok.wait()
+
+    def tokens_b_here():
+        for a in range(N):
+            tok_b.far(a)
+
+    acc[...] = jnp.zeros((EXPERTS, GROUP, 2 * UNITS), F32)
     own_chunks(0)
+    spread(1)
+    tok_a.near(3)
+    tok_a.near(1)
+    spread(2)
+    tok_b.start(tok)
+    relay(0)
     own_chunks(1)
-    relay(0)
-    tokens.near(3)
-    tokens.near(1)
-    tokens.relay(0)
+    tok_a.relay(0)
+    tok_a.near(2)
+    tok_a.relay(3)
+    tok_a.relay(1)
     hand_over(0)
+    relay(1)
+    tok_b.near(3)
+    tok_b.near(1)
     own_chunks(2)
-    tokens.near(2)
-    relay(1)
+    tok_a.relay(2)
     hand_over_far(0)
+    tok_b.relay(0)
+    tok_b.near(2)
+    hand_over(1)
+    tokens_a_here()
+    all_from_partner(0)
+    products(0, 0)
+    tok_b.relay(3)
+    tok_b.relay(1)
+    relay(2)
     down_own(1)
     down_own(2)
-    tokens.relay(3)
-    tokens.relay(1)
-    hand_over(1)
-    relay(2)
-    tokens.relay(2)
-    down_relay(0)
-    own_tok.wait()
-    for a in range(N):
-        tokens.far(a)
-
-    def products(w):
-        def one(q, carry):
-            span = pl.ds(pl.multiple_of(q * QUARTER, 256), QUARTER)
-            left = xs[:, :, :, span].reshape(GROUP, QUARTER)
-            right = jnp.concatenate([wg[2 * w, span, :], wg[2 * w + 1, span, :]], axis=1)
-            acc[w] += jnp.dot(left, right, preferred_element_type=F32)
-            return carry
-
-        acc[w] = jnp.zeros((GROUP, 2 * UNITS), F32)
-        lax.fori_loop(0, N, one, 0)
-
-    from_partner(0)
-    products(0)
     hand_over_far(1)
-    from_partner(1)
-    products(1)
+    tok_b.relay(2)
+    all_from_partner(1)
+    products(1, 0)
+    tokens_b_here()
+    products(0, 2)
+    products(1, 2)
+
     hand_over(2)
     hand_over_far(2)
-    from_partner(2)
-    products(2)
+    for cy in (y, before, after, across):
+        from_partner(2, cy)
+    products(2, 0)
+    products(2, 2)
 
     for bx in range(N):
         rows = slice(bx * N * ROWS, (bx + 1) * N * ROWS)
@@ -345,11 +378,14 @@
             value = value * column[:, 2 + k : 3 + k]
             hb[x, z, rows, k * UNITS : (k + 1) * UNITS] = value.astype(BF16)
 
-    def down_products(half, a):
-        rows = pl.ds(half * GROUP // 2, GROUP // 2)
+    near_blocks = [(a, b) for a in (0, 3, 1) for b in (0, 3, 1)]
+    far_blocks = [(2, 0), (0, 2), (2, 3), (3, 2), (2, 1), (1, 2), (2, 2)]
+
+    def down_products(i, blocks, start):
+        rows = pl.ds(i * GROUP // 2, GROUP // 2)
         left, right = [], []
-        for b in range(N):
-            bx, bz = hidden.block(half, a, b)
+        for a, b in blocks:
+            bx, bz = ring(x, a), ring(z, b)
             one, two = hb[bx, bz, rows, 0:UNITS], hb[bx, bz, rows, UNITS : 2 * UNITS]
             for w in range(EXPERTS):
                 left.append(one * mask[0, w, rows, :] + two * mask[1, w, rows, :])
@@ -358,36 +394,75 @@
             jnp.concatenate(left, axis=1), jnp.concatenate(right, axis=1),
             (((1,), (1,)), ((), ())), preferred_element_type=F32,
         )
-        total_ref[rows, :] = more if a == 0 else total_ref[rows, :] + more
-
-    hidden.start()
+        if start:
+            total_ref[rows, :] = more
+            return
+        more = more + total_ref[rows, :]
+        for cy in range(N):
+            piece = more[:, cy * 128 : (cy + 1) * 128].astype(BF16)
+            ob[2 * i : 2 * i + 2, :, cy, :, :] = piece.reshape(2, N, ROWS, 128)
+
+    spot = back.at[xl, :, :, pl.ds(pl.multiple_of(t_index * 128, 128), 128)]
+
+    def give_back(i):
+        for near in (1, 0):
+            bx = 2 * i + lax.rem(x + near, 2)
+            for d in (1, 3, 2, 0):
+                if near == 0 and d == 0:
+                    continue
+                bz = ring(z, d)
+                send(ob.at[bx, bz], spot, osem, device(y, bx, bz, c))
+
+        @pl.when(i == xh)
+        def _():
+            pltpu.make_async_copy(ob.at[x, z], spot, osem).start()
+
+        @pl.when(i != xh)
+        def _():
+            pltpu.make_async_remote_copy(
+                src_ref=ob.at[ring(x, 2), z],
+                dst_ref=spot,
+                send_sem=fsem,
+                recv_sem=osem,
+                device_id=device(y, ring(x, 2), z, c),
+                device_id_type=MESH,
+            ).start()
+
+    hid_a.start()
+    hid_b.start()
+    hid_a.near(3)
+    hid_a.near(1)
+    down_relay(0)
+    hid_a.relay(0)
+    hid_a.near(2)
+    hid_b.near(3)
+    hid_b.near(1)
     down_relay(1)
-    hidden.near(3)
-    hidden.near(1)
-    hidden.relay(0)
+    hid_a.relay(3)
+    hid_a.relay(1)
+    hid_b.relay(0)
     down_relay(2)
-    hidden.near(2)
+    hid_b.near(2)
+    hid_a.relay(2)
+    hid_b.relay(3)
+    hid_b.relay(1)
     for w in range(EXPERTS):
         down_far(w)
-    hidden.relay(3)
-    hidden.relay(1)
-    hidden.relay(2)
+    hid_b.relay(2)
     for w in range(EXPERTS):
         own_down[w].wait()
         for cy in (y, before, after, across):
             down_wait(w, cy, 1 - c)
-    for a in (0, 3, 1, 2):
-        hidden.far(a)
-        for half in range(2):
-            down_products(half, a)
-
-    for cy in range(N):
-        piece = total_ref[:, cy * 128 : (cy + 1) * 128].astype(BF16)
-        ob[:, :, cy, :, :] = piece.reshape(N, N, ROWS, 128)
-    spot = back.at[xl, :, :, pl.ds(pl.multiple_of(t_index * 128, 128), 128)]
-    for (dx, dz), to in zip(PLANE, peers):
-        send(ob.at[ring(x, dx), ring(z, dz)], spot, osem, to)
-    pltpu.make_async_copy(ob.at[x, z], spot, osem).start()
+    down_products(0, near_blocks, True)
+    for a in range(N):
+        hid_a.far(a)
+    down_products(0, far_blocks, False)
+    give_back(0)
+    down_products(1, near_blocks, True)
+    for a in range(N):
+        hid_b.far(a)
+    down_products(1, far_blocks, False)
+    give_back(1)
     arrived(back, osem)
     result = jnp.dot(
         back[...].reshape(2 * N * ROWS, 8 * 128), order_ref[...], preferred_element_type=F32
@@ -400,11 +475,12 @@
 
     for cp in sends:
         cp.wait_send()
+    arrived(ob.at[ring(x, 2), z], fsem)
     for w in range(EXPERTS):
         arrived(wg.at[0:2, 0 : 15 * DEPTH, :], asend.at[w])
 
 
-SENDS = 146
+SENDS = 212
 
 
 def local(tokens, expert_ids, gate_scores, gate_weight, up_weight, down_weight):
@@ -433,8 +509,9 @@
             dma((EXPERTS, 2)),
             dma((EXPERTS, 16)),
             dma((EXPERTS, N, 2)),
-            dma((2, N, N)),
-            dma((2, N, N)),
+            dma((2, 2, N, N)),
+            dma((2, 2, N, N)),
+            dma,
             dma,
             dma,
             dma,

time: 125 us -> 113 us (0.904)
  Pallas kernels: 123 us -> 110 us
    pallas_call x1, Pallas kernels: 123 us -> 110 us  [local(): pl.pallas_call(kernel, out_shape=jax.ShapeDtypeStruct((ROWS, D), BF16), i...]
where the time goes in v4:
time: 113 us; the launch traced here: 112 us
  Pallas kernels  110 us (97%)
  local copies, waits for them, and re-layouts  1.82 us (2%)
    pallas_call x1, Pallas kernels, local(): pl.pallas_call(kernel, out_shape=jax.ShapeDtypeStruct((ROWS, D), BF16), i...  110 us

profile of v4, /device:TPU:1, one launch (start us, length us, event | category | flops | bytes accessed | tf_op | source)
XLA Modules:
  0.0 112.0 jit_solution(1335083244681721697)
XLA Ops:
  0.0 110.2 %relay_experts.1 = bf16[32,7168]{1,0:T(8,128)(2,1)} custom-call(bf16[32,7168]{1,0:T(8,128)(2,1)} %tok.1, s32[2,256]{1,0:T(2,128)} %bitcast.2, s32[2,256]{1,0:T(2,128)} %bitcast.3, bf16[3,56,2048]{2,1,0:T(8,128)(2,1)} %gate.1, bf16[3,56,2048]{2,1,0:T(8,128)(2,1)} %up.1, bf16[3,56,2048]{2,1,0:T(8,128)(2,1)} %down.1), custom_call_target="tpu_custom_call" | custom-call | tf_op jit(solution)/shard_map/relay_experts/pallas_call | solution.py:490
  110.2 1.8 %copy.8 = bf16[32,7168]{1,0:T(8,128)(2,1)} copy(bf16[32,7168]{1,0:T(8,128)(2,1)} %relay_experts.1) | data formatting | bytes 917504

commit v5 on v4

--- a/solution.py
+++ b/solution.py
@@ -92,7 +92,7 @@
     for w in range(EXPERTS):
         for i, ref in enumerate((gate, up)):
             pltpu.make_async_copy(
-                ref.at[w, :, columns(x, z)], wg.at[2 * w + i, own_rows, :], arecv.at[w, xl]
+                ref.at[w, :, columns(x, z)], wg.at[i, w, own_rows, :], arecv.at[min(w, 1), xl]
             ).start()
 
     def down_piece(w, cy, cc, cols=slice(None)):
@@ -130,15 +130,17 @@
         down_wait(w, across, c)
         down_pass(w, across, partner)
 
-    def spread(w):
+    sets = (pl.ds(0, 1), pl.ds(1, EXPERTS - 1))
+
+    def spread(k):
         for (dx, dz), to in zip(PLANE, peers):
             cols = columns(ring(x, dx), ring(z, dz))
             for i, ref in enumerate((gate, up)):
                 pltpu.make_async_remote_copy(
-                    src_ref=ref.at[w, :, cols],
-                    dst_ref=wg.at[2 * w + i, own_rows, :],
-                    send_sem=asend.at[w],
-                    recv_sem=arecv.at[w, xl],
+                    src_ref=ref.at[sets[k], :, cols],
+                    dst_ref=wg.at[i, sets[k], own_rows, :],
+                    send_sem=asend.at[k],
+                    recv_sem=arecv.at[k, xl],
                     device_id=to,
                     device_id_type=MESH,
                 ).start()
@@ -146,7 +148,7 @@
     def chunk(w, cy, cx, cc):
         k = cy * 4 + cx * 2 + cc
         rows = pl.ds(pl.multiple_of(k * CHUNK, CHUNK), CHUNK)
-        return wg.at[pl.ds(2 * w, 2), rows, :], wrecv.at[w, k]
+        return wg.at[:, w, rows, :], wrecv.at[w, k]
 
     def pass_on(w, cy, cx, to):
         ref, sem = chunk(w, cy, cx, c)
@@ -156,10 +158,16 @@
         ref, sem = chunk(w, cy, cx, cc)
         arrived(ref, sem)
 
+    def spread_here(k, cx):
+        rows = pl.ds(pl.multiple_of((y * 4 + cx * 2 + c) * CHUNK, CHUNK), CHUNK)
+        arrived(wg.at[:, sets[k], rows, :], arecv.at[k, cx])
+
     def own_chunks(w):
-        arrived(chunk(w, y, 0, c)[0], arecv.at[w, 0])
+        if w < 2:
+            spread_here(w, 0)
         pass_on(w, y, 0, north)
-        arrived(chunk(w, y, 1, c)[0], arecv.at[w, 1])
+        if w < 2:
+            spread_here(w, 1)
         pass_on(w, y, 1, south)
         pass_on(w, y, 1, north)
         pass_on(w, y, 0, south)
@@ -295,7 +303,7 @@
     def quarter(w, q):
         span = pl.ds(pl.multiple_of(q * QUARTER, 256), QUARTER)
         left = xs[:, :, :, span].reshape(GROUP, QUARTER)
-        right = jnp.concatenate([wg[2 * w, span, :], wg[2 * w + 1, span, :]], axis=1)
+        right = jnp.concatenate([wg[0, w, span, :], wg[1, w, span, :]], axis=1)
         acc[w] += jnp.dot(left, right, preferred_element_type=F32)
 
     def products(w, first):
@@ -323,7 +331,6 @@
     spread(1)
     tok_a.near(3)
     tok_a.near(1)
-    spread(2)
     tok_b.start(tok)
     relay(0)
     own_chunks(1)
@@ -476,8 +483,8 @@
     for cp in sends:
         cp.wait_send()
     arrived(ob.at[ring(x, 2), z], fsem)
-    for w in range(EXPERTS):
-        arrived(wg.at[0:2, 0 : 15 * DEPTH, :], asend.at[w])
+    for k in range(2):
+        arrived(wg.at[:, sets[k], 0 : 15 * DEPTH, :], asend.at[k])
 
 
 SENDS = 212
@@ -494,7 +501,7 @@
         out_specs=vmem,
         scratch_shapes=[
             pltpu.VMEM((N, N, ROWS, D), BF16),
-            pltpu.VMEM((2 * EXPERTS, D, UNITS), BF16),
+            pltpu.VMEM((2, EXPERTS, D, UNITS), BF16),
             pltpu.VMEM((EXPERTS, N, 128, FF), BF16),
             pltpu.VMEM((EXPERTS, GROUP, 2 * UNITS), F32),
             pltpu.VMEM((N, N, GROUP, 2 * UNITS), BF16),
@@ -505,8 +512,8 @@
             pltpu.VMEM((8 * 128, SPAN), BF16),
             pltpu.VMEM((2, 8, 256), F32),
             dma((SENDS,)),
-            dma((EXPERTS,)),
-            dma((EXPERTS, 2)),
+            dma((2,)),
+            dma((2, 2)),
             dma((EXPERTS, 16)),
             dma((EXPERTS, N, 2)),
             dma((2, 2, N, N)),

time: 113 us -> 113 us (level)
  no operation moved by 1% of the time
where the time goes in v5:
time: 113 us; the launch traced here: 112 us
  Pallas kernels  110 us (97%)
  local copies, waits for them, and re-layouts  1.82 us (2%)
    pallas_call x1, Pallas kernels, local(): pl.pallas_call(kernel, out_shape=jax.ShapeDtypeStruct((ROWS, D), BF16), i...  110 us

profile of v5, /device:TPU:1, one launch (start us, length us, event | category | flops | bytes accessed | tf_op | source)
XLA Modules:
  0.0 111.5 jit_solution(10837867369153390991)
XLA Ops:
  0.0 109.7 %relay_experts.1 = bf16[32,7168]{1,0:T(8,128)(2,1)} custom-call(bf16[32,7168]{1,0:T(8,128)(2,1)} %tok.1, s32[2,256]{1,0:T(2,128)} %bitcast.2, s32[2,256]{1,0:T(2,128)} %bitcast.3, bf16[3,56,2048]{2,1,0:T(8,128)(2,1)} %gate.1, bf16[3,56,2048]{2,1,0:T(8,128)(2,1)} %up.1, bf16[3,56,2048]{2,1,0:T(8,128)(2,1)} %down.1), custom_call_target="tpu_custom_call" | custom-call | tf_op jit(solution)/shard_map/relay_experts/pallas_call | solution.py:497
  109.7 1.8 %copy.8 = bf16[32,7168]{1,0:T(8,128)(2,1)} copy(bf16[32,7168]{1,0:T(8,128)(2,1)} %relay_experts.1) | data formatting | bytes 917504

commit v6 on v5

--- a/solution.py
+++ b/solution.py
@@ -348,12 +348,12 @@
     tok_b.relay(0)
     tok_b.near(2)
     hand_over(1)
+    tok_b.relay(3)
+    tok_b.relay(1)
+    relay(2)
     tokens_a_here()
     all_from_partner(0)
     products(0, 0)
-    tok_b.relay(3)
-    tok_b.relay(1)
-    relay(2)
     down_own(1)
     down_own(2)
     hand_over_far(1)
@@ -361,15 +361,21 @@
     all_from_partner(1)
     products(1, 0)
     tokens_b_here()
-    products(0, 2)
-    products(1, 2)
+    def second_half(n, carry):
+        quarter(lax.div(n, 2), 2 + lax.rem(n, 2))
+        return carry
+
+    lax.fori_loop(0, 4, second_half, 0)
 
     hand_over(2)
     hand_over_far(2)
     for cy in (y, before, after, across):
         from_partner(2, cy)
-    products(2, 0)
-    products(2, 2)
+    def third(n, carry):
+        quarter(2, n)
+        return carry
+
+    lax.fori_loop(0, 4, third, 0)
 
     for bx in range(N):
         rows = slice(bx * N * ROWS, (bx + 1) * N * ROWS)

time: 113 us -> 113 us (level)
  no operation moved by 1% of the time
where the time goes in v6:
time: 113 us; the launch traced here: 111 us
  Pallas kernels  109 us (96%)
  local copies, waits for them, and re-layouts  1.82 us (2%)
    pallas_call x1, Pallas kernels, local(): pl.pallas_call(kernel, out_shape=jax.ShapeDtypeStruct((ROWS, D), BF16), i...  109 us

profile of v6, /device:TPU:1, one launch (start us, length us, event | category | flops | bytes accessed | tf_op | source)
XLA Modules:
  0.0 111.2 jit_solution(1523239249203459327)
XLA Ops:
  0.0 109.4 %relay_experts.1 = bf16[32,7168]{1,0:T(8,128)(2,1)} custom-call(bf16[32,7168]{1,0:T(8,128)(2,1)} %tok.1, s32[2,256]{1,0:T(2,128)} %bitcast.2, s32[2,256]{1,0:T(2,128)} %bitcast.3, bf16[3,56,2048]{2,1,0:T(8,128)(2,1)} %gate.1, bf16[3,56,2048]{2,1,0:T(8,128)(2,1)} %up.1, bf16[3,56,2048]{2,1,0:T(8,128)(2,1)} %down.1), custom_call_target="tpu_custom_call" | custom-call | tf_op jit(solution)/shard_map/relay_experts/pallas_call | solution.py:503
  109.4 1.8 %copy.8 = bf16[32,7168]{1,0:T(8,128)(2,1)} copy(bf16[32,7168]{1,0:T(8,128)(2,1)} %relay_experts.1) | data formatting | bytes 917504
